TPU v7x, 32 devices: a whole 2x2x4 slice. The times are simulated.
32 devices in a mesh: groups: 2 (over x), row: 16 (over z, y, core).
Axes of the slice: x: 2, y: 2, z: 4, core: 2. Of those that a mesh axis runs over, the one named last changes fastest.
Arguments:
- orbitals: bfloat16 [4096, 512], P(('groups', 'row')), parts along dimension 0, may hold values from -1.296875 to 1.296875
- basis: bfloat16 [4096, 1024], P(('groups', 'row')), parts along dimension 0, may hold values from -0.1875 to 0.1875
- kernel: bfloat16 [4096, 2048], P(('groups', 'row')), parts along dimension 0, may hold values from -6 to 6
Outputs:
- exchange_matrix: float32 [2048, 1024], P('groups', 'row'), parts along dimension 0
There are 2 independent parts, one for each index of `groups`. A program takes and returns all parts, laid end to end along the dimension named above; each array names one. Nothing has to cross between parts.
All inputs are finite; a program needn't handle non-finite values.
Results may differ from a plain program's by a relative error of at most 0.0041.
Values may be sent and summed in bfloat16 or wider, within the bound.
A program may use at most 128 MiB of HBM per device.

v0:
```python
import jax
import jax.numpy as jnp
from jax import lax
from jax.sharding import PartitionSpec as P


def shards(orbitals, basis, kernel):
    density = lax.dot_general(
        orbitals,
        lax.all_gather(orbitals, "row", axis=0, tiled=True),
        (((1,), (1,)), ((), ())),
        preferred_element_type=jnp.float32,
    )
    weighted = (density * kernel.astype(jnp.float32)).astype(jnp.bfloat16)
    whole_basis = lax.all_gather(basis, "row", axis=0, tiled=True)
    applied = jnp.dot(weighted, whole_basis, preferred_element_type=jnp.float32).astype(
        jnp.bfloat16
    )
    received = lax.all_to_all(applied, "row", split_axis=1, concat_axis=0, tiled=True)
    exchange_matrix = lax.dot_general(
        whole_basis, received, (((0,), (0,)), ((), ())), preferred_element_type=jnp.float32
    )
    return exchange_matrix


def solution(mesh):
    return jax.shard_map(
        shards,
        mesh=mesh,
        in_specs=(
            P(("groups", "row"), None),
            P(("groups", "row"), None),
            P(("groups", "row"), None),
        ),
        out_specs=P("groups", "row"),
        check_vma=False,
    )
```

profile of v0, /device:TPU:0, one launch (start us, length us, event | category | flops | bytes accessed | tf_op | source)
XLA Modules:
  0.0 133.2 jit_solution(10812226006285130068)
XLA Ops:
  6.5 0.0 all-gather.3.cloned.1.call-start
  6.5 0.7 all-gather.3.cloned.1.call-update
  7.3 0.0 all-gather.5.cloned.1.call-start
  7.3 0.7 all-gather.5.cloned.1.call-update
  8.0 45.7 %all-gather.3.cloned.1.call-done = bf16[2048,512]{1,0:T(8,128)(2,1)} async-done(((bf16[128,512]{1,0:T(8,128)(2,1)}), bf16[2048,512]{1,0:T(8,128)(2,1)}) %all-gather.3.cloned.1.call-update) | async-done | bytes 2097168 | tf_op jit(solution)/shard_map/all_gather | solution.py:10
  53.7 51.3 %all-gather.5.cloned.1.call-done = bf16[2048,1024]{1,0:T(8,128)(2,1)} async-done(((bf16[128,1024]{1,0:T(8,128)(2,1)}), bf16[2048,1024]{1,0:T(8,128)(2,1)}) %all-gather.5.cloned.1.call-update) | async-done | bytes 4194320 | tf_op jit(solution)/shard_map/all_gather | solution.py:15
  105.0 4.4 %convolution_convert_fusion = bf16[128,1024]{1,0:T(8,128)(2,1)S(1)} fusion(bf16[2048,1024]{1,0:T(8,128)(2,1)} %all-gather.5.cloned.1.call-done, bf16[128,512]{1,0:T(8,128)(2,1)} %param.3, bf16[2048,512]{1,0:T(8,128)(2,1)} %all-gather.3.cloned.1.call-done, bf16[128,2048]{1,0:T(8,128)(2,1)} %param.5), kind=kOutput, calls=%fused_computation.2 | convolution fusion | flops 806223872 | bytes 7208960 | tf_op jit(solution)/shard_map/dot_general | solution.py:16
  109.4 0.2 copy.4
  109.6 13.1 %all_to_all.19 = bf16[128,16,64]{0,2,1:T(8,128)(2,1)S(1)} all-to-all(bf16[128,16,64]{0,2,1:T(8,128)(2,1)S(1)} %bitcast.15), channel_id=1, replica_groups=mesh['groups'=2,'row'=16] {'row'}, dimensions={1} | all-to-all | bytes 524288 | tf_op jit(solution)/shard_map/all_to_all | solution.py:19
  122.6 3.7 %convolution_bitcast_fusion = f32[1024,64]{0,1:T(8,128)} fusion(bf16[2048,1024]{1,0:T(8,128)(2,1)} %all-gather.5.cloned.1.call-done, bf16[128,16,64]{0,2,1:T(8,128)(2,1)S(1)} %all_to_all.19), kind=kOutput, calls=%fused_computation.3 | convolution fusion | flops 268435456 | bytes 4718592 | tf_op jit(solution)/shard_map/dot_general | solution.py:20
Async XLA Ops:
  6.5 47.2 %all-gather.3.cloned.1.call-start = ((), (), s32[]{:S(2)}) async-start(), calls=%async_computation.1 | async-start | bytes 2228224 | tf_op jit(solution)/shard_map/all_gather | solution.py:10
  7.3 97.7 %all-gather.5.cloned.1.call-start = ((), (), s32[]{:S(2)}) async-start(), calls=%async_computation.2 | async-start | bytes 4456448 | tf_op jit(solution)/shard_map/all_gather | solution.py:15
Sparse Core Ops, SparseCore 0:
  9.5 44.1 all-gather.2
  55.9 49.0 all-gather.4
where the time goes:
time: 133 us
  waiting for transfers between devices  98.4 us (74%)
  between operations  13.4 us (10%)
  blocking collectives  13.1 us (10%)
  matrix products  8.13 us (6%)
    all_gather x1, waiting for transfers between devices, shards(): whole_basis = lax.all_gather(basis, 'row', axis=0, tiled=True)  51.3 us
    all_gather x1, waiting for transfers between devices, shards(): lax.all_gather(orbitals, 'row', axis=0, tiled=True)  45.7 us
    all_to_all x1, blocking collectives, shards(): lax.all_to_all(applied, 'row', split_axis=1, concat_axis=0, tiled=True)  13.1 us
    dot_general x1, matrix products, shards(): jnp.dot(weighted, whole_basis, preferred_element_type=jnp.float32)  4.39 us
    dot_general x1, matrix products, shards(): lax.dot_general(whole_basis, received, (((0,), (0,)), ((), ())), preferre...  3.73 us
  transfers between devices with their start and end apart: 2, of which 2 were waited for; matrix products, arithmetic and copies ran while one was open for 0% of the time, Pallas kernels for 0%

commit v1 on v0

v1 whole, which is shorter than its diff:
```python
import functools

import jax
import jax.numpy as jnp
from jax import lax
from jax.experimental import pallas as pl
from jax.experimental.pallas import tpu as pltpu
from jax.sharding import PartitionSpec as P

LANES = 128
MESH = pl.DeviceIdType.MESH


def layout(mesh):
    n = mesh.shape["row"]
    try:
        line = mesh.devices[0]
        places = [tuple(d.coords) + (d.core_on_chip,) for d in line]
    except AttributeError:
        return n, 1, 1
    cores = len({p[-1] for p in places})
    axes = [a for a in range(3) if len({p[a] for p in places}) > 1]
    sizes = {a: len({p[a] for p in places}) for a in axes}
    for axis_z in axes:
        rest = [a for a in axes if a != axis_z]
        if len(rest) > 1 or (rest and sizes[rest[0]] != 2):
            continue
        y_size = sizes[rest[0]] if rest else 1
        z0 = min(p[axis_z] for p in places)
        y0 = min(p[rest[0]] for p in places) if rest else 0
        found = [
            ((p[axis_z] - z0) * y_size + (p[rest[0]] - y0 if rest else 0)) * cores + p[-1]
            for p in places
        ]
        if found == list(range(n)):
            return sizes[axis_z], y_size, cores
    return n, 1, 1


def kernel(
    dims, o_in, b_in, k_in, out_ref,
    o_all, b_all, k_v, w, app_t, got, in_sem, send_sem, recv_sem, a2a_send, a2a_recv,
):
    Z, Y, C = dims
    n = Z * Y * C
    units = Z * Y
    parts = 3
    rows = o_in.shape[0]
    half_cols = b_all.shape[-1]
    groups = half_cols // LANES
    cw = app_t.shape[0] * app_t.shape[1] // n
    per = LANES // cw

    me = lax.axis_index("row")
    c = me % C
    y = (me // C) % Y
    z = me // (C * Y)
    peer_y = (Y - 1) - y

    def index(zz, yy, cc):
        return (zz * Y + yy) * C + cc

    up_dev = index(jnp.minimum(z + 1, Z - 1), y, c)
    down_dev = index(jnp.maximum(z - 1, 0), y, c)
    y_dev = index(z, peer_y, c)
    sib_dev = index(z, y, (C - 1) - c)
    has_up = z < Z - 1
    has_down = z > 0

    def chunk(i, p):
        return o_all.at[i] if p == 0 else b_all.at[p - 1, i]

    def copy(i, p, kind):
        dev = (up_dev, down_dev, y_dev, sib_dev)[kind]
        return pltpu.make_async_remote_copy(
            src_ref=chunk(i, p),
            dst_ref=chunk(i, p),
            send_sem=send_sem.at[kind, p, i // C],
            recv_sem=recv_sem.at[p, i],
            device_id={"row": dev},
            device_id_type=MESH,
        )

    def wait_recv(i, p):
        copy(i, p, 3).wait_recv()

    loads = [pltpu.make_async_copy(o_in, o_all.at[me], in_sem.at[0])]
    for g in range(2 * groups):
        h, s = g % 2, g // 2
        loads.append(
            pltpu.make_async_copy(
                b_in.at[:, pl.ds(g * LANES, LANES)],
                b_all.at[h, me, :, pl.ds(s * LANES, LANES)],
                in_sem.at[1 + g],
            )
        )
    k_load = pltpu.make_async_copy(k_in, k_v, in_sem.at[1 + 2 * groups])
    for load in loads:
        load.start()
    k_load.start()

    barrier = pltpu.get_barrier_semaphore()

    def greet(dev):
        pl.semaphore_signal(barrier, inc=1, device_id={"row": dev}, device_id_type=MESH)

    pl.when(has_up)(lambda: greet(up_dev))
    pl.when(has_down)(lambda: greet(down_dev))
    if Y > 1:
        greet(y_dev)
    if C > 1:
        greet(sib_dev)
    others = (Y > 1) + (C > 1)
    pl.semaphore_wait(barrier, others + has_up.astype(jnp.int32) + has_down.astype(jnp.int32))

    def spread(i, p, up=False, down=False, across=False):
        if up:
            pl.when(has_up)(lambda: copy(i, p, 0).start())
        if down:
            pl.when(has_down)(lambda: copy(i, p, 1).start())
        if across and Y > 1:
            copy(i, p, 2).start()
        if C > 1:
            copy(i, p, 3).start()

    def own(p):
        if p == 0:
            loads[0].wait()
        else:
            for g in range(2 * groups):
                if g % 2 == p - 1:
                    loads[1 + g].wait()
        spread(me, p, up=True, down=True, across=True)

    def along(p, t):
        def low():
            i = index(z - t, y, c)
            wait_recv(i, p)
            spread(i, p, up=True, across=True)

        def high():
            i = index(z + t, y, c)
            wait_recv(i, p)
            spread(i, p, down=True, across=True)

        pl.when(z - t >= 0)(low)
        pl.when(z + t < Z)(high)

    def across(p, t):
        def one(zz):
            i = index(zz, peer_y, c)
            wait_recv(i, p)
            spread(i, p)

        if t == 0:
            one(z)
        else:
            pl.when(z - t >= 0)(lambda: one(z - t))
            pl.when(z + t < Z)(lambda: one(z + t))

    events = []
    for p in range(parts):
        events.append((p * (Z - 1) + 0.5 * (p > 0), p, functools.partial(own, p)))
        for t in range(1, Z):
            events.append((p * (Z - 1) + t, p, functools.partial(along, p, t)))
        if Y > 1:
            for t in range(Z):
                events.append((p * Z + t + 1 + 0.6 * (t > 0), p, functools.partial(across, p, t)))
    events.sort(key=lambda e: e[0])
    last = [max(k for k, e in enumerate(events) if e[1] == p) for p in range(parts)]

    def wait_sibling(p, u):
        if C > 1:
            wait_recv(u * C + (C - 1) - c, p)

    def weigh(u):
        if u == 0:
            k_load.wait()
        wait_sibling(0, u)
        cols = pl.ds(u * C * rows, C * rows)
        block = o_all[u * C:(u + 1) * C].reshape(C * rows, o_all.shape[-1])
        density = lax.dot_general(
            o_all[me], block, (((1,), (1,)), ((), ())), preferred_element_type=jnp.float32
        )
        w[:, cols] = (density * k_v[:, cols].astype(jnp.float32)).astype(jnp.bfloat16)

    wide = 2 * LANES if groups % 2 == 0 else LANES
    depth = min(n, max(1, 2048 // rows))

    def apply(h, j):
        if j == 0:
            for u in range(units):
                wait_sibling(1 + h, u)
        cols = pl.ds(j * wide, wide)

        def term(q):
            block = b_all[h, pl.ds(q * depth, depth), :, cols].reshape(depth * rows, wide)
            return jnp.dot(
                w[:, pl.ds(pl.multiple_of(q * depth * rows, LANES), depth * rows)],
                block,
                preferred_element_type=jnp.float32,
            )

        if n == depth:
            total = term(0)
        else:
            total = lax.fori_loop(
                0, n // depth, lambda q, a: a + term(q), jnp.zeros((rows, wide), jnp.float32)
            )
        app_t[h, cols, :] = total.astype(jnp.bfloat16).T

    count = n // 2

    def exchange(h, q):
        qq = (q + me) % count
        s, e = qq // per, qq % per
        d = (2 * s + h) * per + e
        off = pl.multiple_of(s * LANES + e * cw, 16)
        return d, pltpu.make_async_remote_copy(
            src_ref=app_t.at[h, pl.ds(off, cw), :],
            dst_ref=got.at[:, pl.ds(pl.multiple_of(me * rows, LANES), rows)],
            send_sem=a2a_send.at[h, q],
            recv_sem=a2a_recv.at[me],
            device_id={"row": d},
            device_id_type=MESH,
        ), pltpu.make_async_copy(
            app_t.at[h, pl.ds(off, cw), :],
            got.at[:, pl.ds(pl.multiple_of(me * rows, LANES), rows)],
            a2a_recv.at[me],
        )

    def hand_out(h):
        for q in range(count):
            d, remote, local = exchange(h, q)
            pl.when(d != me)(lambda: remote.start())
            pl.when(d == me)(lambda: local.start())

    work = {p: [] for p in range(parts)}
    for u in range(units):
        work[0].append(functools.partial(weigh, u))
    for h in range(2):
        for j in range(half_cols // wide):
            work[1 + h].append(functools.partial(apply, h, j))
        work[1 + h].append(functools.partial(hand_out, h))

    queue = []
    for k, (_, _, event) in enumerate(events):
        event()
        if queue:
            queue.pop(0)()
        for p in range(parts):
            if last[p] == k:
                queue.extend(work[p])
    for item in queue:
        item()

    for src in range(n):
        pltpu.make_async_copy(
            got.at[:, pl.ds(src * rows, rows)], got.at[:, pl.ds(src * rows, rows)], a2a_recv.at[src]
        ).wait()
    for h in range(2):
        for j in range(half_cols // wide):
            cols = pl.ds(j * wide, wide)

            def term(q):
                block = b_all[h, pl.ds(q * depth, depth), :, cols].reshape(depth * rows, wide)
                return jnp.dot(
                    got[:, pl.ds(pl.multiple_of(q * depth * rows, LANES), depth * rows)],
                    block,
                    preferred_element_type=jnp.float32,
                )

            if n == depth:
                total = term(0)
            else:
                total = lax.fori_loop(
                    0, n // depth, lambda q, a: a + term(q), jnp.zeros((cw, wide), jnp.float32)
                )
            for v in range(wide // LANES):
                g = 2 * (j * (wide // LANES) + v) + h
                out_ref[pl.ds(g * LANES, LANES), :] = total[:, v * LANES:(v + 1) * LANES].T

    for h in range(2):
        for q in range(count):
            d, remote, _ = exchange(h, q)
            pl.when(d != me)(lambda: remote.wait_send())
    for p in range(parts):
        for zz in range(Z):
            i = index(zz, y, c)
            pl.when(jnp.logical_and(has_up, zz <= z))(lambda: copy(i, p, 0).wait_send())
            pl.when(jnp.logical_and(has_down, zz >= z))(lambda: copy(i, p, 1).wait_send())
            if Y > 1:
                copy(i, p, 2).wait_send()
        if C > 1:
            for u in range(units):
                copy(u * C + c, p, 3).wait_send()


def shards(dims, orbitals, basis, kernel_block):
    Z, Y, C = dims
    n = Z * Y * C
    rows, nocc = orbitals.shape
    nb = basis.shape[1]
    points = kernel_block.shape[1]
    half = nb // 2
    cw = nb // n
    bf16 = jnp.bfloat16
    any_space = pl.BlockSpec(memory_space=pl.ANY)
    return pl.pallas_call(
        functools.partial(kernel, dims),
        out_shape=jax.ShapeDtypeStruct((nb, cw), jnp.float32),
        in_specs=[any_space] * 3,
        out_specs=pl.BlockSpec(memory_space=pltpu.VMEM),
        scratch_shapes=[
            pltpu.VMEM((n, rows, nocc), bf16),
            pltpu.VMEM((2, n, rows, half), bf16),
            pltpu.VMEM((rows, points), bf16),
            pltpu.VMEM((rows, points), bf16),
            pltpu.VMEM((2, half, rows), bf16),
            pltpu.VMEM((cw, points), bf16),
            pltpu.SemaphoreType.DMA((2 + nb // LANES,)),
            pltpu.SemaphoreType.DMA((4, 3, Z * Y)),
            pltpu.SemaphoreType.DMA((3, n)),
            pltpu.SemaphoreType.DMA((2, n // 2)),
            pltpu.SemaphoreType.DMA((n,)),
        ],
        compiler_params=pltpu.CompilerParams(
            collective_id=0, has_side_effects=True, vmem_limit_bytes=60 * 1024 * 1024
        ),
    )(orbitals, basis, kernel_block)


def solution(mesh):
    spec = P(("groups", "row"), None)
    return jax.shard_map(
        functools.partial(shards, layout(mesh)),
        mesh=mesh,
        in_specs=(spec, spec, spec),
        out_specs=P("groups", "row"),
        check_vma=False,
    )
```

time: 133 us -> 57.1 us (0.43)
  the two profiles are of different devices: /device:TPU:0 before, /device:TPU:12 now
where the time goes in v1:
time: 57.1 us; the launch traced here: 57 us
  Pallas kernels  55 us (96%)
  local copies, waits for them, and re-layouts  1.93 us (3%)
    pallas_call x1, Pallas kernels, shards(): pl.pallas_call(functools.partial(kernel, dims), out_shape=jax.ShapeDtypeS...  55 us
    pallas_call x1, local copies, waits for them, and re-layouts, shards(): pl.pallas_call(functools.partial(kernel, dims), out_shape=jax.ShapeDtypeS...  1.93 us

profile of v1, /device:TPU:12, one launch (start us, length us, event | category | flops | bytes accessed | tf_op | source)
XLA Modules:
  0.0 57.0 jit_solution(568240908463350959)
XLA Ops:
  0.0 55.0 %shard_map.37 = f32[1024,64]{1,0:T(8,128)} custom-call(bf16[128,512]{1,0:T(8,128)(2,1)} %o_in.1, bf16[128,1024]{1,0:T(8,128)(2,1)} %b_in.1, bf16[128,2048]{1,0:T(8,128)(2,1)} %k_in.1), custom_call_target="tpu_custom_call" | custom-call | tf_op jit(solution)/shard_map/pallas_call | solution.py:309
  55.0 1.9 %copy.4 = f32[1024,64]{0,1:T(8,128)} copy(f32[1024,64]{1,0:T(8,128)} %shard_map.37) | data formatting | bytes 524288 | tf_op jit(solution)/shard_map/pallas_call | solution.py:309

commit v2 on v1

--- a/solution.py
+++ b/solution.py
@@ -113,13 +113,30 @@
     others = (Y > 1) + (C > 1)
     pl.semaphore_wait(barrier, others + has_up.astype(jnp.int32) + has_down.astype(jnp.int32))
 
-    def spread(i, p, up=False, down=False, across=False):
+    relays = Y > 1 and Z >= 4
+    both, either = jnp.logical_and, jnp.logical_or
+
+    def goes_across(zz, p):
+        if not relays:
+            return True
+        turn = c == p % C
+        end = either(both(both(z == 0, zz == 1), turn), both(both(z == Z - 1, zz == Z - 2), turn))
+        beside = either(both(z == 1, zz == 0), both(z == Z - 2, zz == Z - 1))
+        return jnp.logical_not(either(end, beside))
+
+    def relay_up(p):
+        return either(z == 0, both(z == Z - 2, c == p % C))
+
+    def relay_down(p):
+        return either(z == Z - 1, both(z == 1, c == p % C))
+
+    def spread(i, zz, p, up=False, down=False, across=False):
         if up:
             pl.when(has_up)(lambda: copy(i, p, 0).start())
         if down:
             pl.when(has_down)(lambda: copy(i, p, 1).start())
         if across and Y > 1:
-            copy(i, p, 2).start()
+            pl.when(goes_across(zz, p))(lambda: copy(i, p, 2).start())
         if C > 1:
             copy(i, p, 3).start()
 
@@ -130,18 +147,18 @@
             for g in range(2 * groups):
                 if g % 2 == p - 1:
                     loads[1 + g].wait()
-        spread(me, p, up=True, down=True, across=True)
+        spread(me, z, p, up=True, down=True, across=True)
 
     def along(p, t):
         def low():
             i = index(z - t, y, c)
             wait_recv(i, p)
-            spread(i, p, up=True, across=True)
+            spread(i, z - t, p, up=True, across=True)
 
         def high():
             i = index(z + t, y, c)
             wait_recv(i, p)
-            spread(i, p, down=True, across=True)
+            spread(i, z + t, p, down=True, across=True)
 
         pl.when(z - t >= 0)(low)
         pl.when(z + t < Z)(high)
@@ -150,7 +167,10 @@
         def one(zz):
             i = index(zz, peer_y, c)
             wait_recv(i, p)
-            spread(i, p)
+            if relays and t == 0:
+                pl.when(relay_up(p))(lambda: copy(i, p, 0).start())
+                pl.when(relay_down(p))(lambda: copy(i, p, 1).start())
+            spread(i, zz, p)
 
         if t == 0:
             one(z)
@@ -160,12 +180,13 @@
 
     events = []
     for p in range(parts):
-        events.append((p * (Z - 1) + 0.5 * (p > 0), p, functools.partial(own, p)))
+        base = p * ((Z - 0.5) if relays else (Z if Y > 1 else max(Z - 1, 1)))
+        events.append((base - 0.7 * (p > 0), p, functools.partial(own, p)))
         for t in range(1, Z):
-            events.append((p * (Z - 1) + t, p, functools.partial(along, p, t)))
+            events.append((base + t, p, functools.partial(along, p, t)))
         if Y > 1:
             for t in range(Z):
-                events.append((p * Z + t + 1 + 0.6 * (t > 0), p, functools.partial(across, p, t)))
+                events.append((base + t + 1 + 0.6 * (t > 0), p, functools.partial(across, p, t)))
     events.sort(key=lambda e: e[0])
     last = [max(k for k, e in enumerate(events) if e[1] == p) for p in range(parts)]
 
@@ -290,7 +311,11 @@
             pl.when(jnp.logical_and(has_up, zz <= z))(lambda: copy(i, p, 0).wait_send())
             pl.when(jnp.logical_and(has_down, zz >= z))(lambda: copy(i, p, 1).wait_send())
             if Y > 1:
-                copy(i, p, 2).wait_send()
+                pl.when(goes_across(zz, p))(lambda: copy(i, p, 2).wait_send())
+        if relays:
+            i = index(z, peer_y, c)
+            pl.when(relay_up(p))(lambda: copy(i, p, 0).wait_send())
+            pl.when(relay_down(p))(lambda: copy(i, p, 1).wait_send())
         if C > 1:
             for u in range(units):
                 copy(u * C + c, p, 3).wait_send()

time: 57.1 us -> 53 us (0.928)
  Pallas kernels: 55 us -> 50.5 us
    pallas_call x1, Pallas kernels: 55 us -> 50.5 us  [shards(): pl.pallas_call(functools.partial(kernel, dims), out_shape=jax.ShapeDtypeS...]
where the time goes in v2:
time: 53 us; the launch traced here: 52.4 us
  Pallas kernels  50.5 us (95%)
  local copies, waits for them, and re-layouts  1.93 us (4%)
    pallas_call x1, Pallas kernels, shards(): pl.pallas_call(functools.partial(kernel, dims), out_shape=jax.ShapeDtypeS...  50.5 us
    pallas_call x1, local copies, waits for them, and re-layouts, shards(): pl.pallas_call(functools.partial(kernel, dims), out_shape=jax.ShapeDtypeS...  1.93 us

profile of v2, /device:TPU:12, one launch (start us, length us, event | category | flops | bytes accessed | tf_op | source)
XLA Modules:
  0.0 52.4 jit_solution(6477728790267047814)
XLA Ops:
  0.0 50.5 %shard_map.37 = f32[1024,64]{1,0:T(8,128)} custom-call(bf16[128,512]{1,0:T(8,128)(2,1)} %o_in.1, bf16[128,1024]{1,0:T(8,128)(2,1)} %b_in.1, bf16[128,2048]{1,0:T(8,128)(2,1)} %k_in.1), custom_call_target="tpu_custom_call" | custom-call | tf_op jit(solution)/shard_map/pallas_call | solution.py:334
  50.5 1.9 %copy.4 = f32[1024,64]{0,1:T(8,128)} copy(f32[1024,64]{1,0:T(8,128)} %shard_map.37) | data formatting | bytes 524288 | tf_op jit(solution)/shard_map/pallas_call | solution.py:334

commit v3 on v2

--- a/solution.py
+++ b/solution.py
@@ -8,6 +8,7 @@
 from jax.sharding import PartitionSpec as P
 
 LANES = 128
+LEAD, LEAD_Y, LATE, ACROSS = (0, 7, 7), (0, 7, 7), 0, (2.1, 5.6)
 MESH = pl.DeviceIdType.MESH
 
 
@@ -147,7 +148,13 @@
             for g in range(2 * groups):
                 if g % 2 == p - 1:
                     loads[1 + g].wait()
-        spread(me, z, p, up=True, down=True, across=True)
+        pl.when(has_up)(lambda: copy(me, p, 0).start())
+        pl.when(has_down)(lambda: copy(me, p, 1).start())
+        if C > 1:
+            copy(me, p, 3).start()
+
+    def own_across(p):
+        copy(me, p, 2).start()
 
     def along(p, t):
         def low():
@@ -178,15 +185,17 @@
             pl.when(z - t >= 0)(lambda: one(z - t))
             pl.when(z + t < Z)(lambda: one(z + t))
 
+    stride = (Z - 0.5) if relays else (Z if Y > 1 else max(Z - 1, 1))
     events = []
     for p in range(parts):
-        base = p * ((Z - 0.5) if relays else (Z if Y > 1 else max(Z - 1, 1)))
-        events.append((base - 0.7 * (p > 0), p, functools.partial(own, p)))
+        base = p * stride
+        events.append((base - LEAD[p], p, functools.partial(own, p)))
         for t in range(1, Z):
-            events.append((base + t, p, functools.partial(along, p, t)))
+            events.append((base + t + LATE * (t > 1), p, functools.partial(along, p, t)))
         if Y > 1:
+            events.append((base - LEAD_Y[p] + 0.01, p, functools.partial(own_across, p)))
             for t in range(Z):
-                events.append((base + t + 1 + 0.6 * (t > 0), p, functools.partial(across, p, t)))
+                events.append((base + t + ACROSS[t > 0], p, functools.partial(across, p, t)))
     events.sort(key=lambda e: e[0])
     last = [max(k for k, e in enumerate(events) if e[1] == p) for p in range(parts)]
 
@@ -299,7 +308,7 @@
                 )
             for v in range(wide // LANES):
                 g = 2 * (j * (wide // LANES) + v) + h
-                out_ref[pl.ds(g * LANES, LANES), :] = total[:, v * LANES:(v + 1) * LANES].T
+                out_ref[:, pl.ds(g * LANES, LANES)] = total[:, v * LANES:(v + 1) * LANES]
 
     for h in range(2):
         for q in range(count):
@@ -333,7 +342,7 @@
     any_space = pl.BlockSpec(memory_space=pl.ANY)
     return pl.pallas_call(
         functools.partial(kernel, dims),
-        out_shape=jax.ShapeDtypeStruct((nb, cw), jnp.float32),
+        out_shape=jax.ShapeDtypeStruct((cw, nb), jnp.float32),
         in_specs=[any_space] * 3,
         out_specs=pl.BlockSpec(memory_space=pltpu.VMEM),
         scratch_shapes=[
@@ -352,7 +361,7 @@
         compiler_params=pltpu.CompilerParams(
             collective_id=0, has_side_effects=True, vmem_limit_bytes=60 * 1024 * 1024
         ),
-    )(orbitals, basis, kernel_block)
+    )(orbitals, basis, kernel_block).T
 
 
 def solution(mesh):

time: 53 us -> 50.5 us (0.953)
  Pallas kernels: 50.5 us -> 47.8 us
    pallas_call x1, Pallas kernels: 50.5 us -> 47.8 us  [shards(): pl.pallas_call(functools.partial(kernel, dims), out_shape=jax.ShapeDtypeS...]
    pallas_call x1 -> x0, local copies, waits for them, and re-layouts: 1.93 us -> none  [shards(): pl.pallas_call(functools.partial(kernel, dims), out_shape=jax.ShapeDtypeS...]
    unnamed x0 -> x1, local copies, waits for them, and re-layouts: none -> 1.67 us
where the time goes in v3:
time: 50.5 us; the launch traced here: 49.5 us
  Pallas kernels  47.8 us (95%)
  local copies, waits for them, and re-layouts  1.67 us (3%)
    pallas_call x1, Pallas kernels, shards(): pl.pallas_call(functools.partial(kernel, dims), out_shape=jax.ShapeDtypeS...  47.8 us
    unnamed x1, local copies, waits for them, and re-layouts  1.67 us

profile of v3, /device:TPU:12, one launch (start us, length us, event | category | flops | bytes accessed | tf_op | source)
XLA Modules:
  0.0 49.5 jit_solution(11088506550724070594)
XLA Ops:
  0.0 47.8 %shard_map.37 = f32[64,1024]{1,0:T(8,128)} custom-call(bf16[128,512]{1,0:T(8,128)(2,1)} %o_in.1, bf16[128,1024]{1,0:T(8,128)(2,1)} %b_in.1, bf16[128,2048]{1,0:T(8,128)(2,1)} %k_in.1), custom_call_target="tpu_custom_call" | custom-call | tf_op jit(solution)/shard_map/pallas_call | solution.py:343
  47.8 1.7 %copy.5 = f32[1024,64]{0,1:T(8,128)} copy(f32[1024,64]{0,1:T(8,128)} %bitcast.1) | data formatting | bytes 524288
